TPU v7x, 32 devices: a whole 2x2x4 slice. The times are simulated.
32 devices in a mesh: order: 8 (over z, x), chan: 4 (over y, core).
Axes of the slice: x: 2, y: 2, z: 4, core: 2. Of those that a mesh axis runs over, the one named last changes fastest.
Arguments:
- cotangent: bfloat16 [248, 240, 1, 2, 1024], P('order', None, None, None, 'chan'), may hold values from -0.59765625 to 0.59765625
- stored_coefficients: bfloat16 [248, 240, 1, 2, 1024], P('order', None, None, None, 'chan'), may hold values from -0.29882812 to 0.29882812
- weights: bfloat16 [248, 1024, 1024], P('order', 'chan'), may hold values from -0.1875 to 0.1875
- order_table: int32 [248], replicated, may hold values from 0 to 240, as said below
- degree_table: int32 [248], replicated, may hold values from 0 to 240, as said below
Outputs:
- input_gradient: bfloat16 [248, 240, 1, 2, 1024], P('order', None, None, None, 'chan')
- mixing_gradient: bfloat16 [248, 1024, 1024], P('order', 'chan')
Inputs may be any that keep to these rules, and one draw needn't show every extreme that they name: `order_table`: each order 0 to 239 stands in exactly one slot; every other slot holds 240, meaning empty. `degree_table`: each degree 0 to 239 stands in exactly one slot; every other slot holds 240, meaning empty.
All inputs are finite; a program needn't handle non-finite values.
Results may differ from a plain program's by a relative error of at most 0.008.
Values may be sent and summed in bfloat16 or wider, within the bound.
A program may use at most 192 MiB of HBM per device.

v0:
```python
import jax
import jax.numpy as jnp
from jax import lax
from jax.sharding import PartitionSpec as P


def legendre_rows(orders, degree_range, latitude_count):
    order_real = orders.astype(jnp.float32)[:, None]
    angles = jnp.pi * (jnp.arange(latitude_count).astype(jnp.float32) + 0.5) / latitude_count
    cosine = jnp.cos(angles)[None, :]
    sine = jnp.sin(angles)[None, :]
    counter = jnp.arange(1, degree_range + 1).astype(jnp.float32)
    factors = jnp.log((2.0 * counter - 1.0) / (2.0 * counter))
    below = (counter[None, :] <= order_real).astype(jnp.float32)
    log_start = 0.5 * (
        jnp.log((2.0 * order_real + 1.0) / (4.0 * jnp.pi))
        + jnp.sum(below * factors[None, :], axis=1, keepdims=True)
    )
    parity = 1.0 - 2.0 * (orders % 2).astype(jnp.float32)[:, None]
    start = parity * jnp.exp(log_start + order_real * jnp.log(sine))

    def advance(carry, degree):
        latest, before = carry
        level = degree.astype(jnp.float32)
        upper = jnp.sqrt(
            jnp.maximum(4.0 * level * level - 1.0, 0.0)
            / jnp.maximum(level * level - order_real * order_real, 1.0)
        )
        lower = jnp.sqrt(
            jnp.maximum((level - 1.0) * (level - 1.0) - order_real * order_real, 0.0)
            / jnp.maximum(4.0 * (level - 1.0) * (level - 1.0) - 1.0, 1.0)
        )
        grown = upper * (cosine * latest - lower * before)
        fresh = jnp.where(
            level == order_real, start, jnp.where(level > order_real, grown, jnp.zeros_like(grown))
        )
        return ((fresh, latest), fresh)

    zeros = jnp.zeros((orders.shape[0], latitude_count), jnp.float32)
    unused_result, stacked = lax.scan(advance, (zeros, zeros), jnp.arange(degree_range))
    return jnp.transpose(stacked, (1, 0, 2))


def quadrature(latitude_count):
    angles = jnp.pi * (jnp.arange(latitude_count).astype(jnp.float32) + 0.5) / latitude_count
    return jnp.pi / latitude_count * jnp.sin(angles)


def per_device(cotangent, stored_coefficients, weights, order_table, degree_table):
    slots, latitude_count, batch_size, unused_result, slot_width = cotangent.shape
    degree_range = stored_coefficients.shape[1]
    peers = lax.axis_size("order")
    position = lax.axis_index("order")
    mine = lax.dynamic_slice_in_dim(order_table, position * slots, slots)
    table = legendre_rows(mine, degree_range, latitude_count)
    table_halfprecision = table.astype(jnp.bfloat16)
    flat_cotangent = cotangent.reshape(slots, latitude_count, batch_size * 2 * slot_width)
    adjoint = jnp.einsum(
        "slj,sjf->slf", table_halfprecision, flat_cotangent, preferred_element_type=jnp.float32
    ).astype(jnp.bfloat16)
    adjoint = adjoint.reshape(slots, degree_range, batch_size * 2, slot_width)
    active_mask = jnp.arange(degree_range)[None, :] >= mine[:, None]
    masked_values = stored_coefficients.reshape(
        slots, degree_range, batch_size * 2, slot_width
    ) * active_mask[:, :, None, None].astype(jnp.bfloat16)
    clipped = jnp.minimum(degree_table, degree_range - 1)
    valid = (degree_table[None, :] >= mine[:, None]) & (degree_table[None, :] < degree_range)
    valid_bf = valid.astype(jnp.bfloat16)

    def pack_rows(source):
        picked = jnp.take(source, clipped, axis=1) * valid_bf[:, :, None, None]
        return picked.reshape(slots, peers, slots, batch_size * 2, source.shape[3])

    send_adjoint = pack_rows(adjoint)
    send_saved = pack_rows(masked_values)
    recv_saved, recv_adjoint = (
        lax.all_to_all(send_saved, "order", split_axis=1, concat_axis=1, tiled=True),
        lax.all_to_all(send_adjoint, "order", split_axis=1, concat_axis=1, tiled=True),
    )
    recv_adjoint = lax.all_gather(recv_adjoint, "chan", axis=4, tiled=True)
    mixing_gradient = jnp.einsum(
        "sntrc,sntrd->tcd", recv_saved, recv_adjoint, preferred_element_type=jnp.float32
    ).astype(jnp.bfloat16)
    coefficient_gradient = jnp.einsum(
        "sntrd,tcd->sntrc", recv_adjoint, weights, preferred_element_type=jnp.float32
    ).astype(jnp.bfloat16)
    returned = lax.all_to_all(
        coefficient_gradient, "order", split_axis=1, concat_axis=1, tiled=True
    )
    returned = returned.reshape(slots, peers * slots, batch_size * 2 * slot_width)
    picked_table = jnp.take(table_halfprecision, clipped, axis=1) * valid_bf[:, :, None]
    summed = jnp.einsum("skj,skf->sjf", picked_table, returned, preferred_element_type=jnp.float32)
    quad = quadrature(latitude_count)
    input_gradient = (summed * quad[None, :, None]).astype(jnp.bfloat16)
    return (
        input_gradient.reshape(slots, latitude_count, batch_size, 2, slot_width),
        mixing_gradient,
    )


def solution(mesh):
    return jax.shard_map(
        per_device,
        mesh=mesh,
        in_specs=(
            P("order", None, None, None, "chan"),
            P("order", None, None, None, "chan"),
            P("order", "chan", None),
            P(),
            P(),
        ),
        out_specs=(P("order", None, None, None, "chan"), P("order", "chan", None)),
        check_vma=False,
    )
```

profile of v0, /device:TPU:0, one launch (start us, length us, event | category | flops | bytes accessed | tf_op | source)
XLA Modules:
  0.0 1297.3 jit_solution(11286440266197965360)
XLA Ops:
  7.3 0.8 fusion.22
  9.7 491.0 %while.18 = (s32[]{:T(128)}, f32[31,240]{1,0:T(8,128)S(1)}, f32[31,240]{1,0:T(8,128)S(1)}, bf16[240,31,240]{2,1,0:T(8,128)(2,1)}, s32[240]{0:T(256)S(1)}, /*inde...) while((s32[]{:T(128)}, f32[31,240]{1,0:T(8,128)S(1)}, ...), condition=%wide.region_2.3_spmd.clone, body=%wide.region_1.2_spmd.clone.sunk | while | flops 75383 | bytes 156779 | solution.py:40
  15.2 0.7 bitcast_dynamic-update-slice_fusion.2
  31.5 0.7 bitcast_dynamic-update-slice_fusion.2
  64.3 0.7 bitcast_dynamic-update-slice_fusion.2
  86.8 0.7 bitcast_dynamic-update-slice_fusion.2
  95.0 0.7 bitcast_dynamic-update-slice_fusion.2
  113.4 0.7 bitcast_dynamic-update-slice_fusion.2
  121.6 0.7 bitcast_dynamic-update-slice_fusion.2
  135.9 0.7 bitcast_dynamic-update-slice_fusion.2
  176.8 0.7 bitcast_dynamic-update-slice_fusion.2
  195.2 0.7 bitcast_dynamic-update-slice_fusion.2
  234.1 0.7 bitcast_dynamic-update-slice_fusion.2
  244.3 0.7 bitcast_dynamic-update-slice_fusion.2
  275.0 0.7 bitcast_dynamic-update-slice_fusion.2
  283.2 0.7 bitcast_dynamic-update-slice_fusion.2
  309.8 0.7 bitcast_dynamic-update-slice_fusion.2
  365.0 0.7 bitcast_dynamic-update-slice_fusion.2
  381.4 0.7 bitcast_dynamic-update-slice_fusion.2
  391.6 0.7 bitcast_dynamic-update-slice_fusion.2
  430.5 0.7 bitcast_dynamic-update-slice_fusion.2
  440.7 0.7 bitcast_dynamic-update-slice_fusion.2
  448.9 0.7 bitcast_dynamic-update-slice_fusion.2
  463.2 0.7 bitcast_dynamic-update-slice_fusion.2
  479.6 0.7 bitcast_dynamic-update-slice_fusion.2
  496.0 0.7 bitcast_dynamic-update-slice_fusion.2
  500.8 17.3 %reshape.244 = bf16[31,240,512]{2,1,0:T(8,128)(2,1)} reshape(bf16[31,240,1,2,256]{4,3,2,1,0:T(2,128)(2,1)} %param.9) | data formatting | bytes 15237120 | tf_op jit(solution)/shard_map/reshape | solution.py:57
  518.1 12.3 convolution_convert_fusion
  530.4 16.2 %reshape.245 = bf16[31,240,2,256]{3,2,1,0:T(2,128)(2,1)} reshape(bf16[31,240,512]{2,1,0:T(8,128)(2,1)} %convolution_convert_fusion) | data formatting | bytes 15237120 | tf_op jit(solution)/shard_map/reshape | solution.py:61
  546.6 28.1 %gather_fusion.1 = bf16[248,31,2,256]{3,2,1,0:T(2,128)(2,1)} fusion(bf16[31,240,2,256]{3,2,1,0:T(2,128)(2,1)} %reshape.245, s32[1024]{0:T(1024)S(1)} %pad_clamp_fusion), kind=kCustom, calls=%fused_computation.clone | custom fusion | bytes 15746016 | tf_op jit(solution)/shard_map/jit(_take)/gather | solution.py:71
  574.7 11.6 bitcast_multiply_fusion.2
  586.3 39.2 %gather_fusion.2 = bf16[248,31,2,256]{3,2,1,0:T(2,128)(2,1)} fusion(bf16[31,240,2,256]{3,2,1,0:T(2,128)(2,1)} %bitcast_multiply_fusion.2, s32[1024]{0:T(1024)S(1)} %pad_clamp_fusion), kind=kCustom, calls=%fused_computation.1.clone | custom fusion | bytes 15746016 | tf_op jit(solution)/shard_map/jit(_take)/gather | solution.py:71
  625.6 20.7 %bitcast_multiply_fusion = (bf16[31,248,2,256]{3,2,0,1:T(2,128)(2,1)}, bf16[31,248,2,256]{3,2,0,1:T(2,128)(2,1)S(1)}) fusion(bf16[248,31,2,256]{3,2,1,0:T(2,128)(2,1)} %gather_fusion.2, pred[248]{0:T(512)(128)(4,1)S(1)} %get-tuple-element.223, bf16[31,248]{0,1:T(8,128)(2,1)S(1)} %and_convert_fusion, bf16[248,31,2,256]{3,2,1,0:T(2,128)(2,1)} %gather_fusion.1), kind=kLoop, calls=%fused_computation.22 | loop fusion | flops 15745024 | bytes 31505672 | tf_op jit(solution)/shard_map/mul | solution.py:71
  646.3 179.9 %all_to_all.15 = bf16[31,8,31,2,256]{4,3,0,2,1:T(2,128)(2,1)S(1)} all-to-all(bf16[31,8,31,2,256]{4,3,0,2,1:T(2,128)(2,1)S(1)} %bitcast.58), channel_id=1, replica_groups=mesh['order'=8,'chan'=4] {'order'}, dimensions={1} | all-to-all | bytes 15745024 | tf_op jit(solution)/shard_map/all_to_all | solution.py:78
  826.2 5.4 copy.23
  831.6 7.7 copy.28
  839.2 5.1 all-to-all-start.2
  844.4 6.8 gather_fusion
  851.7 6.0 bitcast_multiply_fusion.3
  857.8 166.1 %all-gather.2.cloned.1.call-done = bf16[31,8,31,2,1024]{4,1,3,0,2:T(8,128)(2,1)} async-done(((bf16[31,8,31,2,256]{4,1,3,0,2:T(8,128)(2,1)}), bf16[31,8,31,2,1024]{4,1,3,0,2:T(8,128)(2,1)}) %all-gather.2.cloned.1.call-update) | async-done | bytes 31490064 | tf_op jit(solution)/shard_map/all_gather | solution.py:80
  1023.9 19.6 %convert_bitcast_fusion = bf16[31,8,31,2,256]{4,1,3,0,2:T(8,128)(2,1)} fusion(bf16[31,8,31,2,1024]{4,1,3,0,2:T(8,128)(2,1)} %all-gather.2.cloned.1.call-done, bf16[31,256,1024]{2,1,0:T(8,128)(2,1)} %param.11), kind=kOutput, calls=%fused_computation.25 | convolution fusion | flops 8065388544 | bytes 55615488 | tf_op jit(solution)/shard_map/sntrd,tcd->sntrc/dot_general | solution.py:84
  1043.6 12.8 copy.24
  1056.4 5.5 all-to-all-start.1
  1061.9 23.4 %bitcast_convert_fusion = bf16[31,256,1024]{2,1,0:T(8,128)(2,1)} fusion(bf16[31,8,31,2,1024]{4,1,3,0,2:T(8,128)(2,1)} %all-gather.2.cloned.1.call-done, bf16[31,8,31,2,256]{4,3,2,0,1:T(2,128)(2,1)} %all-to-all-done.2), kind=kOutput, calls=%fused_computation.13 | convolution fusion | flops 8069578752 | bytes 55615488 | tf_op jit(solution)/shard_map/sntrc,sntrd->tcd/dot_general | solution.py:81
  1085.3 149.1 %all-to-all-done.1 = bf16[31,8,31,2,256]{4,3,0,2,1:T(2,128)(2,1)} async-done(((bf16[31,8,31,2,256]{4,3,0,2,1:T(2,128)(2,1)}), bf16[31,8,31,2,256]{4,3,0,2,1:T(2,128)(2,1)}, u32[]{:S(2)}, u32[]{:S(2)}) %all-to-all-start.1) | async-done | bytes 7872544 | tf_op jit(solution)/shard_map/all_to_all | solution.py:87
  1234.4 17.8 %reshape.284 = bf16[31,248,512]{2,0,1:T(8,128)(2,1)} reshape(bf16[31,8,31,2,256]{4,3,0,2,1:T(2,128)(2,1)} %all-to-all-done.1) | data formatting | bytes 15745024 | tf_op jit(solution)/shard_map/reshape | solution.py:90
  1252.2 21.6 %multiply_convert_fusion = bf16[31,240,512]{2,1,0:T(8,128)(2,1)} fusion(bf16[31,248,512]{2,0,1:T(8,128)(2,1)} %reshape.284, f32[240]{0:T(256)S(1)} %copy-done.1, bf16[31,248,240]{2,0,1:T(8,128)(2,1)} %bitcast_multiply_fusion.3), kind=kOutput, calls=%fused_computation.20 | convolution fusion | flops 1897021440 | bytes 19182272 | tf_op jit(solution)/shard_map/skj,skf->sjf/dot_general | solution.py:92
  1273.8 16.2 %reshape.248 = bf16[31,240,1,2,256]{4,3,1,0,2:T(2,128)(2,1)} reshape(bf16[31,240,512]{2,1,0:T(8,128)(2,1)} %multiply_convert_fusion) | data formatting | bytes 15237120 | tf_op jit(solution)/shard_map/reshape | solution.py:96
  (1199 shorter events, 312.3 us)
Async XLA Ops:
  7.2 1016.8 %all-gather.2.cloned.1.call-start = ((), (), s32[]{:S(2)}) async-start(), calls=%async_computation.3 | async-start | bytes 39362560 | tf_op jit(solution)/shard_map/all_gather | solution.py:80
  586.3 39.2 %copy-start = (s32[248]{0:T(256)S(1)}, s32[248]{0:T(256)}, u32[]{:S(2)}) copy-start(s32[248]{0:T(256)} %param.13) | copy-start | bytes 2980
  839.2 217.1 %all-to-all-start.2 = ((bf16[31,8,31,2,256]{4,3,2,0,1:T(2,128)(2,1)}), bf16[31,8,31,2,256]{4,3,2,0,1:T(2,128)(2,1)}, u32[]{:S(2)}, u32[]{:S(2)}) async-start(bf16[31,8,31,2,256]{4,3,2,0,1:T(2,128)(2,1)} %copy.28), calls=%async_computation.2 | async-start | bytes 15745024 | tf_op jit(solution)/shard_map/all_to_all | solution.py:77
  1056.4 178.0 %all-to-all-start.1 = ((bf16[31,8,31,2,256]{4,3,0,2,1:T(2,128)(2,1)}), bf16[31,8,31,2,256]{4,3,0,2,1:T(2,128)(2,1)}, u32[]{:S(2)}, u32[]{:S(2)}) async-start(bf16[31,8,31,2,256]{4,3,0,2,1:T(2,128)(2,1)} %copy.24), calls=%async_computation.1 | async-start | bytes 15745024 | tf_op jit(solution)/shard_map/all_to_all | solution.py:87
  1085.3 166.9 %copy-start.1 = (f32[240]{0:T(256)S(1)}, f32[240]{0:T(256)}, u32[]{:S(2)}) copy-start(f32[240]{0:T(256)} %fusion.18) | copy-start | bytes 2884
Sparse Core Ops, SparseCore 0:
  831.7 192.1 all-gather.1
where the time goes:
time: 1310 us; the launch traced here: 1300 us
  waiting for transfers between devices  315 us (24%)
  local copies, waits for them, and re-layouts  307 us (23%)
  other arithmetic  229 us (17%)
  blocking collectives  180 us (14%)
  loops' own time  164 us (13%)
  matrix products  76.9 us (6%)
  between operations  14.5 us (1%)
    all_to_all x1, blocking collectives, per_device(): lax.all_to_all(send_adjoint, 'order', split_axis=1, concat_axis=1, tiled=...  180 us
    dynamic_update_slice x240, other arithmetic, legendre_rows(): lax.scan(advance, (zeros, zeros), jnp.arange(degree_range))  169 us
    all_gather x1, waiting for transfers between devices, per_device(): recv_adjoint = lax.all_gather(recv_adjoint, 'chan', axis=4, tiled=True)  166 us
    another operation x1, loops' own time, legendre_rows(): lax.scan(advance, (zeros, zeros), jnp.arange(degree_range))  164 us
    all_to_all x1, waiting for transfers between devices, per_device(): lax.all_to_all(coefficient_gradient, 'order', split_axis=1, concat_axis=1...  149 us
    dynamic_slice x240, local copies, waits for them, and re-layouts, legendre_rows(): lax.scan(advance, (zeros, zeros), jnp.arange(degree_range))  140 us
    gather x2, local copies, waits for them, and re-layouts, pack_rows(): picked = jnp.take(source, clipped, axis=1) * valid_bf[:, :, None, None]  67.3 us
  transfers between devices with their start and end apart: 3, of which 2 were waited for; matrix products, arithmetic and copies ran while one was open for 6% of the time, Pallas kernels for 0%

commit v1 on v0

--- a/solution.py
+++ b/solution.py
@@ -2,6 +2,16 @@
 import jax.numpy as jnp
 from jax import lax
 from jax.sharding import PartitionSpec as P
+
+fit_regions = lambda u: jnp.concatenate(
+    lax.all_to_all(
+        jnp.stack(jnp.split(u, lax.axis_size("order"), axis=1), axis=0),
+        concat_axis=0,
+        axis_name="order",
+        split_axis=0,
+    ),
+    axis=1,
+)
 
 
 def legendre_rows(orders, degree_range, latitude_count):
@@ -84,9 +94,7 @@
     coefficient_gradient = jnp.einsum(
         "sntrd,tcd->sntrc", recv_adjoint, weights, preferred_element_type=jnp.float32
     ).astype(jnp.bfloat16)
-    returned = lax.all_to_all(
-        coefficient_gradient, "order", split_axis=1, concat_axis=1, tiled=True
-    )
+    returned = fit_regions(coefficient_gradient)
     returned = returned.reshape(slots, peers * slots, batch_size * 2 * slot_width)
     picked_table = jnp.take(table_halfprecision, clipped, axis=1) * valid_bf[:, :, None]
     summed = jnp.einsum("skj,skf->sjf", picked_table, returned, preferred_element_type=jnp.float32)

time: 1310 us -> 1340 us (1.023)
  local copies, waits for them, and re-layouts: 307 us -> 344 us
    split x0 -> x1, local copies, waits for them, and re-layouts: none -> 27.5 us  [jnp.split(u, lax.axis_size('order'), axis=1)]
    another operation x1 -> x4, local copies, waits for them, and re-layouts: 0.01 us -> 26.7 us  [the longest x1 17.9 us: per_device(): returned.reshape(slots, peers * slots, batch_size * 2 * slot_width)]
  transfers between devices with their start and end apart: 3 -> 3, of which waited for: 2 -> 2; matrix products, arithmetic and copies ran while one was open for 6% -> 8% of each run, Pallas kernels for 0% -> 0%
where the time goes in v1:
time: 1340 us; the launch traced here: 1330 us
  local copies, waits for them, and re-layouts  344 us (26%)
  waiting for transfers between devices  315 us (24%)
  other arithmetic  230 us (17%)
  blocking collectives  180 us (13%)
  loops' own time  163 us (12%)
  matrix products  69.2 us (5%)
  between operations  14.5 us (1%)
    all_to_all x1, blocking collectives, per_device(): lax.all_to_all(send_adjoint, 'order', split_axis=1, concat_axis=1, tiled=...  180 us
    dynamic_update_slice x240, other arithmetic, legendre_rows(): lax.scan(advance, (zeros, zeros), jnp.arange(degree_range))  169 us
    all_gather x1, waiting for transfers between devices, per_device(): recv_adjoint = lax.all_gather(recv_adjoint, 'chan', axis=4, tiled=True)  166 us
    another operation x1, loops' own time, legendre_rows(): lax.scan(advance, (zeros, zeros), jnp.arange(degree_range))  163 us
    all_to_all x1, waiting for transfers between devices, lax.all_to_all(jnp.stack(jnp.split(u, lax.axis_size('order'), axis=1), ax...  149 us
    dynamic_slice x240, local copies, waits for them, and re-layouts, legendre_rows(): lax.scan(advance, (zeros, zeros), jnp.arange(degree_range))  140 us
    gather x2, local copies, waits for them, and re-layouts, pack_rows(): picked = jnp.take(source, clipped, axis=1) * valid_bf[:, :, None, None]  67.7 us
    split x1, local copies, waits for them, and re-layouts, jnp.split(u, lax.axis_size('order'), axis=1)  27.5 us
  transfers between devices with their start and end apart: 3, of which 2 were waited for; matrix products, arithmetic and copies ran while one was open for 8% of the time, Pallas kernels for 0%

profile of v1, /device:TPU:0, one launch (start us, length us, event | category | flops | bytes accessed | tf_op | source)
XLA Modules:
  0.0 1325.9 jit_solution(6259484131569808004)
XLA Ops:
  8.7 0.8 fusion.21
  9.7 0.8 and_convert_fusion
  10.5 490.0 %while.18 = (s32[]{:T(128)}, f32[31,240]{1,0:T(8,128)S(1)}, f32[31,240]{1,0:T(8,128)S(1)}, bf16[240,31,240]{2,1,0:T(8,128)(2,1)}, s32[240]{0:T(256)S(1)}, /*inde...) while((s32[]{:T(128)}, f32[31,240]{1,0:T(8,128)S(1)}, ...), condition=%wide.region_2.3_spmd.clone, body=%wide.region_1.2_spmd.clone.sunk | while | flops 75383 | bytes 156279 | solution.py:50
  24.1 0.7 bitcast_dynamic-update-slice_fusion.10
  48.6 0.7 bitcast_dynamic-update-slice_fusion.10
  67.0 0.7 bitcast_dynamic-update-slice_fusion.10
  103.8 0.7 bitcast_dynamic-update-slice_fusion.10
  105.8 0.7 bitcast_dynamic-update-slice_fusion.10
  118.1 0.7 bitcast_dynamic-update-slice_fusion.10
  122.2 0.7 bitcast_dynamic-update-slice_fusion.10
  132.4 0.7 bitcast_dynamic-update-slice_fusion.10
  138.5 0.7 bitcast_dynamic-update-slice_fusion.10
  165.0 0.7 bitcast_dynamic-update-slice_fusion.10
  238.5 0.7 bitcast_dynamic-update-slice_fusion.10
  246.7 0.7 bitcast_dynamic-update-slice_fusion.10
  269.2 0.7 bitcast_dynamic-update-slice_fusion.10
  279.4 0.7 bitcast_dynamic-update-slice_fusion.10
  301.8 0.7 bitcast_dynamic-update-slice_fusion.10
  361.0 0.7 bitcast_dynamic-update-slice_fusion.10
  410.0 0.7 bitcast_dynamic-update-slice_fusion.10
  467.2 0.7 bitcast_dynamic-update-slice_fusion.10
  481.5 0.7 bitcast_dynamic-update-slice_fusion.10
  500.6 17.3 %reshape.244 = bf16[31,240,512]{2,1,0:T(8,128)(2,1)} reshape(bf16[31,240,1,2,256]{4,3,2,1,0:T(2,128)(2,1)} %param.9) | data formatting | bytes 15237120 | tf_op jit(solution)/shard_map/reshape | solution.py:67
  517.9 12.3 convolution_convert_fusion
  530.1 16.2 %reshape.245 = bf16[31,240,2,256]{3,2,1,0:T(2,128)(2,1)} reshape(bf16[31,240,512]{2,1,0:T(8,128)(2,1)} %convolution_convert_fusion) | data formatting | bytes 15237120 | tf_op jit(solution)/shard_map/reshape | solution.py:71
  546.4 11.6 bitcast_multiply_fusion.2
  557.9 28.1 %gather_fusion.2 = bf16[248,31,2,256]{3,2,1,0:T(2,128)(2,1)} fusion(bf16[31,240,2,256]{3,2,1,0:T(2,128)(2,1)} %bitcast_multiply_fusion.2, s32[1024]{0:T(1024)S(1)} %pad_clamp_fusion), kind=kCustom, calls=%fused_computation.1.clone | custom fusion | bytes 15746016 | tf_op jit(solution)/shard_map/jit(_take)/gather | solution.py:81
  586.1 39.6 %gather_fusion.1 = bf16[248,31,2,256]{3,2,1,0:T(2,128)(2,1)} fusion(bf16[31,240,2,256]{3,2,1,0:T(2,128)(2,1)} %reshape.245, s32[1024]{0:T(1024)S(1)} %pad_clamp_fusion), kind=kCustom, calls=%fused_computation.clone | custom fusion | bytes 15746016 | tf_op jit(solution)/shard_map/jit(_take)/gather | solution.py:81
  625.7 20.6 %bitcast_multiply_fusion = (bf16[31,248,2,256]{3,2,0,1:T(2,128)(2,1)}, bf16[31,248,2,256]{3,2,0,1:T(2,128)(2,1)S(1)}) fusion(bf16[248,31,2,256]{3,2,1,0:T(2,128)(2,1)} %gather_fusion.2, pred[248]{0:T(512)(128)(4,1)S(1)} %get-tuple-element.245, bf16[31,248]{0,1:T(8,128)(2,1)S(1)} %and_convert_fusion, bf16[248,31,2,256]{3,2,1,0:T(2,128)(2,1)} %gather_fusion.1), kind=kLoop, calls=%fused_computation.22 | loop fusion | flops 15745024 | bytes 31505672 | tf_op jit(solution)/shard_map/mul | solution.py:81
  646.3 179.9 %all_to_all.15 = bf16[31,8,31,2,256]{4,3,0,2,1:T(2,128)(2,1)S(1)} all-to-all(bf16[31,8,31,2,256]{4,3,0,2,1:T(2,128)(2,1)S(1)} %bitcast.76), channel_id=1, replica_groups=mesh['order'=8,'chan'=4] {'order'}, dimensions={1} | all-to-all | bytes 15745024 | tf_op jit(solution)/shard_map/all_to_all | solution.py:88
  826.2 5.3 copy.172
  831.5 7.7 copy.185
  839.2 5.1 all-to-all-start.2
  844.3 6.8 gather_fusion
  851.8 6.0 bitcast_multiply_fusion.3
  857.8 166.1 %all-gather.2.cloned.1.call-done = bf16[31,8,31,2,1024]{4,1,3,0,2:T(8,128)(2,1)} async-done(((bf16[31,8,31,2,256]{4,1,3,0,2:T(8,128)(2,1)}), bf16[31,8,31,2,1024]{4,1,3,0,2:T(8,128)(2,1)}) %all-gather.2.cloned.1.call-update) | async-done | bytes 31490064 | tf_op jit(solution)/shard_map/all_gather | solution.py:90
  1023.9 19.6 %convert_bitcast_fusion = bf16[31,8,31,2,256]{4,1,3,0,2:T(8,128)(2,1)} fusion(bf16[31,8,31,2,1024]{4,1,3,0,2:T(8,128)(2,1)} %all-gather.2.cloned.1.call-done, bf16[31,256,1024]{2,1,0:T(8,128)(2,1)} %param.11), kind=kOutput, calls=%fused_computation.24 | convolution fusion | flops 8065388544 | bytes 55615488 | tf_op jit(solution)/shard_map/sntrd,tcd->sntrc/dot_general | solution.py:94
  1043.5 27.5 %fusion.23 = (bf16[31,1,31,2,256]{4,1,3,0,2:T(2,128)(2,1)S(1)}, bf16[31,1,31,2,256]{4,1,3,0,2:T(2,128)(2,1)S(1)}, bf16[31,1,31,2,256]{4,1,3,0,2:T(2,128)(2,1)S(1...) fusion(bf16[31,8,31,2,256]{4,1,3,0,2:T(8,128)(2,1)} %convert_bi, ...), kind=kLoop, calls=%fused_computation.63 | loop fusion | bytes 15745024 | tf_op jit(solution)/shard_map/split | solution.py:8
  1071.0 1.8 bitcast_dynamic-update-slice_fusion.8
  1072.8 1.8 bitcast_dynamic-update-slice_fusion.7
  1076.3 8.5 copy.181
  1084.8 5.5 all-to-all-start.1
  1090.4 23.4 %bitcast_convert_fusion = bf16[31,256,1024]{2,1,0:T(8,128)(2,1)} fusion(bf16[31,8,31,2,1024]{4,1,3,0,2:T(8,128)(2,1)} %all-gather.2.cloned.1.call-done, bf16[31,8,31,2,256]{4,3,2,0,1:T(2,128)(2,1)} %all-to-all-done.2), kind=kOutput, calls=%fused_computation.13 | convolution fusion | flops 8069578752 | bytes 55615488 | tf_op jit(solution)/shard_map/sntrc,sntrd->tcd/dot_general | solution.py:91
  1113.8 149.1 %all-to-all-done.1 = bf16[8,31,1,31,2,256]{5,4,3,2,1,0:T(2,128)(2,1)} async-done(((bf16[8,31,1,31,2,256]{5,4,3,2,1,0:T(2,128)(2,1)}), bf16[8,31,1,31,2,256]{5,4,3,2,1,0:T(2,128)(2,1)}, u32[]{:S(2)}, u32[]{:S(2)}) %all-to-all-start.1) | async-done | bytes 7872544 | tf_op jit(solution)/shard_map/all_to_all | solution.py:7
  1262.9 7.8 copy.182
  1270.7 17.9 %reshape_reshape.3 = bf16[31,248,512]{2,1,0:T(8,128)(2,1)} reshape(bf16[31,8,1,31,2,256]{5,4,3,1,0,2:T(2,128)(2,1)} %copy.182) | data formatting | bytes 15745024 | tf_op jit(solution)/shard_map/reshape;reshape | solution.py:98
  1288.6 13.9 %multiply_convert_fusion = bf16[31,240,512]{2,1,0:T(8,128)(2,1)} fusion(bf16[31,248,512]{2,1,0:T(8,128)(2,1)} %reshape_reshape.3, f32[240]{0:T(256)S(1)} %copy-done, bf16[31,248,240]{2,0,1:T(8,128)(2,1)} %bitcast_multiply_fusion.3), kind=kOutput, calls=%fused_computation.20 | convolution fusion | flops 1897021440 | bytes 19182272 | tf_op jit(solution)/shard_map/skj,skf->sjf/dot_general | solution.py:100
  1302.5 16.2 %reshape.248 = bf16[31,240,1,2,256]{4,3,1,0,2:T(2,128)(2,1)} reshape(bf16[31,240,512]{2,1,0:T(8,128)(2,1)} %multiply_convert_fusion) | data formatting | bytes 15237120 | tf_op jit(solution)/shard_map/reshape | solution.py:104
  (1207 shorter events, 317.6 us)
Async XLA Ops:
  7.2 1016.7 %all-gather.2.cloned.1.call-start = ((), (), s32[]{:S(2)}) async-start(), calls=%async_computation.3 | async-start | bytes 39362560 | tf_op jit(solution)/shard_map/all_gather | solution.py:90
  839.2 245.6 %all-to-all-start.2 = ((bf16[31,8,31,2,256]{4,3,2,0,1:T(2,128)(2,1)}), bf16[31,8,31,2,256]{4,3,2,0,1:T(2,128)(2,1)}, u32[]{:S(2)}, u32[]{:S(2)}) async-start(bf16[31,8,31,2,256]{4,3,2,0,1:T(2,128)(2,1)} %copy.185), calls=%async_computation.2 | async-start | bytes 15745024 | tf_op jit(solution)/shard_map/all_to_all | solution.py:87
  1084.8 178.0 %all-to-all-start.1 = ((bf16[8,31,1,31,2,256]{5,4,3,2,1,0:T(2,128)(2,1)}), bf16[8,31,1,31,2,256]{5,4,3,2,1,0:T(2,128)(2,1)}, u32[]{:S(2)}, u32[]{:S(2)}) async-start(bf16[8,31,1,31,2,256]{5,4,3,2,1,0:T(2,128)(2,1)} %copy.181), calls=%async_computation.1 | async-start | bytes 15745024 | tf_op jit(solution)/shard_map/all_to_all | solution.py:7
  1270.7 17.9 %copy-start = (f32[240]{0:T(256)S(1)}, f32[240]{0:T(256)}, u32[]{:S(2)}) copy-start(f32[240]{0:T(256)} %fusion.17) | copy-start | bytes 2884
Sparse Core Ops, SparseCore 0:
  831.6 192.1 all-gather.1
